TPU v7x, 32 devices: a whole 2x2x4 slice. The times are simulated.
32 devices in a mesh: seq: 8 (over z, y), head: 4 (over x, core).
Axes of the slice: x: 2, y: 2, z: 4, core: 2. Of those that a mesh axis runs over, the one named last changes fastest.
Arguments:
- tokens: bfloat16 [16384, 1024], P('seq', 'head'), may hold values from -32 to 32
- buckets: int32 [128, 16], P('seq', 'head'), may hold values from 0 to 63, as said below
- w_shared: bfloat16 [1024, 1024], P(None, 'head'), may hold values from -3 to 3
- w_value: bfloat16 [1024, 1024], P(None, 'head'), may hold values from -0.1875 to 0.1875
- w_output: bfloat16 [1024, 1024], P(None, 'head'), may hold values from -0.1875 to 0.1875
Outputs:
- mixed_out: bfloat16 [16384, 1024], P('seq', 'head')
Inputs may be any that keep to these rules, and one draw needn't show every extreme that they name: `buckets`: for each head, the ids 0 to 63 all occur. With the owner of a block in head h being its position in head h's ordering integer-divided by 16, exactly 16 blocks of each head fall to each owner, and over the 4 heads held by one device along `head` the 16 blocks held by one device along `seq` fall at most 8 to any one owner; 8 is reached in every draw.
All inputs are finite; a program needn't handle non-finite values.
Results may differ from a plain program's by a relative error of at most 0.012.
The roundings to bfloat16 on the way count: a program that leaves them out, or rounds other values in their place, can miss the bound.
Values may be sent and summed in bfloat16 or wider, within the bound.
A program may use at most 64 MiB of HBM per device.

v0:
```python
import jax
import jax.numpy as jnp
from jax import lax
from jax.sharding import PartitionSpec as P

DH = 64
BLK = 128


def carried_in(x, axis, combine, identity):
    peers, position = (lax.axis_size(axis), lax.axis_index(axis))
    everything = lax.all_gather(x, axis)
    start = jnp.broadcast_to(jnp.asarray(identity, x.dtype), x.shape)

    def lap(k, before):
        reached = k < position
        new = combine(before, everything[k])
        return jnp.where(reached, new, before)

    return lax.fori_loop(0, peers, lap, start)


def shifted(x, axis, by):
    peers = lax.axis_size(axis)
    return lax.ppermute(x, axis, [(i, (i + by) % peers) for i in range(peers)])


def add_counts(earlier_sum, later_sum):
    return earlier_sum + later_sum


def per_device(tokens, buckets, w_shared, w_value, w_output):
    seq_count = lax.axis_size("seq")
    block_count, head_count = buckets.shape
    row_count = tokens.shape[0]
    item_count = block_count * head_count
    capacity = max(1, item_count // seq_count)
    bucket_count = block_count * seq_count // 2
    gathered = lax.all_gather(tokens, "head", axis=1, tiled=True)
    shared = jnp.dot(gathered, w_shared, preferred_element_type=jnp.float32).astype(jnp.bfloat16)
    values = jnp.dot(gathered, w_value, preferred_element_type=jnp.float32).astype(jnp.bfloat16)
    bucket_ids = jnp.transpose(buckets)
    onehot = (
        bucket_ids[:, :, None] == jnp.arange(bucket_count, dtype=jnp.int32)[None, None, :]
    ).astype(jnp.int32)
    counts = jnp.sum(onehot, axis=1)
    below = carried_in(counts, "seq", add_counts, jnp.zeros_like(counts)).astype(jnp.int32)
    total = lax.psum(counts, "seq")
    bucket_start = jnp.cumsum(total, axis=1) - total
    offset_table = bucket_start + below
    leading = jnp.sum(onehot * offset_table[:, None, :], axis=2)
    matching = bucket_ids[:, :, None] == bucket_ids[:, None, :]
    earlier = jnp.arange(block_count)[None, :] < jnp.arange(block_count)[:, None]
    local_rank = jnp.sum((matching & earlier[None]).astype(jnp.int32), axis=2)
    position = leading + local_rank
    owner_index = (position // block_count).reshape(item_count)
    within = position % block_count
    item_order = jnp.arange(item_count)
    same_owner = owner_index[:, None] == owner_index[None, :]
    slot_index = jnp.sum(
        (same_owner & (item_order[None, :] < item_order[:, None])).astype(jnp.int32), axis=1
    )
    target = owner_index * capacity + slot_index
    grid_index = (jnp.arange(head_count, dtype=jnp.int32)[:, None] * block_count + within).reshape(
        item_count
    )
    shared_blocks = shared.reshape(block_count, BLK, head_count, DH)
    value_blocks = values.reshape(block_count, BLK, head_count, DH)
    payload = jnp.concatenate([shared_blocks, value_blocks], axis=3)
    payload = jnp.transpose(payload, (2, 0, 1, 3)).reshape(item_count, BLK, 2 * DH)
    outbox = jnp.zeros((seq_count * capacity, BLK, 2 * DH), jnp.bfloat16).at[target].set(payload)
    outbox_index = (
        jnp.full((seq_count * capacity,), item_count, jnp.int32).at[target].set(grid_index)
    )
    received, received_index = (
        lax.all_to_all(outbox, "seq", split_axis=0, concat_axis=0, tiled=True),
        lax.all_to_all(outbox_index, "seq", split_axis=0, concat_axis=0, tiled=True),
    )
    owned = jnp.zeros((item_count + 1, BLK, 2 * DH), jnp.bfloat16).at[received_index].set(received)
    owned = owned[:item_count].reshape(head_count, block_count, BLK, 2 * DH)
    final_block = owned[:, block_count - 1]
    trailing_block = shifted(final_block, "seq", 1)
    preceding = jnp.concatenate([trailing_block[:, None], owned[:, : block_count - 1]], axis=1)
    all_keys = jnp.concatenate([preceding, owned], axis=2)
    queries = owned[..., :DH]
    key_float = all_keys[..., :DH].astype(jnp.float32)
    khat = (
        key_float * lax.rsqrt(jnp.mean(key_float * key_float, axis=-1, keepdims=True) + 1e-06)
    ).astype(jnp.bfloat16)
    scores = jnp.einsum(
        "pbqd,pbkd->pbqk", queries, khat, preferred_element_type=jnp.float32
    ) * DH ** (-0.5)
    self_mask = jnp.arange(2 * BLK)[None, :] == jnp.arange(BLK)[:, None] + BLK
    scores = jnp.where(self_mask[None, None], jnp.float32(-100000.0), scores)
    row_max = jnp.max(scores, axis=-1, keepdims=True)
    expo = jnp.exp(scores - row_max)
    weights = (expo / jnp.sum(expo, axis=-1, keepdims=True)).astype(jnp.bfloat16)
    attention = jnp.einsum(
        "pbqk,pbkd->pbqd", weights, all_keys[..., DH:], preferred_element_type=jnp.float32
    ).astype(jnp.bfloat16)
    flat_attention = jnp.concatenate(
        [attention.reshape(item_count, BLK, DH), jnp.zeros((1, BLK, DH), jnp.bfloat16)], axis=0
    )
    replies = flat_attention[received_index]
    answer_rows = lax.all_to_all(replies, "seq", split_axis=0, concat_axis=0, tiled=True)
    returned = answer_rows[target].reshape(head_count, block_count, BLK, DH)
    head_local = jnp.transpose(returned, (1, 2, 0, 3)).reshape(row_count, head_count * DH)
    heads_all = lax.all_gather(head_local, "head", axis=1, tiled=True)
    mixed = tokens.astype(jnp.float32) + jnp.dot(
        heads_all, w_output, preferred_element_type=jnp.float32
    )
    return mixed.astype(jnp.bfloat16)


def solution(mesh):
    return jax.shard_map(
        per_device,
        mesh=mesh,
        in_specs=(
            P("seq", "head"),
            P("seq", "head"),
            P(None, "head"),
            P(None, "head"),
            P(None, "head"),
        ),
        out_specs=P("seq", "head"),
        check_vma=False,
    )
```

profile of v0, /device:TPU:29, one launch (start us, length us, event | category | flops | bytes accessed | tf_op | source)
XLA Modules:
  0.0 228.2 jit_solution(754004636225795833)
XLA Ops:
  6.5 0.7 all-gather.5.cloned.1.call-update
  7.3 0.8 convert_reduce_fusion.2
  8.0 5.6 %psum.7 = s32[4,64]{1,0:T(4,128)S(1)} all-reduce(s32[4,64]{1,0:T(4,128)S(1)} %convert_reduce_fusion.2), channel_id=1, replica_groups=mesh['seq'=8,'head'=4] {'seq'}, use_global_device_ids=true, to_apply=%region_1.2 | all-reduce | flops 256 | bytes 2048 | tf_op jit(solution)/shard_map/psum | solution.py:48
  13.7 0.2 reduce_window_sum.11
  13.9 20.6 %all-gather.1 = s32[8,4,64]{2,1,0:T(4,128)S(1)} all-gather(s32[1,4,64]{2,1,0:T(4,128)S(1)} %bitcast.68), channel_id=2, replica_groups=mesh['seq'=8,'head'=4] {'seq'}, dimensions={0}, use_global_device_ids=true | all-gather | bytes 9216 | tf_op jit(solution)/shard_map/all_gather | solution.py:12
  34.5 0.3 while.14
  34.9 0.9 select_reduce_fusion
  35.7 1.0 convert_reduce_fusion.1
  37.1 0.2 convert_reduce_fusion
  37.3 0.8 scatter_custom_fusion
  38.1 0.7 all_to_all.14
  38.7 7.0 %all-to-all-start = ((s32[8,8,1]{1,2,0:T(1,128)}), s32[8,8,1]{1,2,0:T(1,128)S(1)}, u32[]{:S(2)}, u32[]{:S(2)}) async-start(s32[8,8,1]{1,2,0:T(1,128)} %bitcast.4), calls=%async_computation | async-start | bytes 8192 | tf_op jit(solution)/shard_map/all_to_all | solution.py:77
  45.8 3.5 %convolution_convert_fusion.1 = bf16[2048,256]{1,0:T(8,128)(2,1)S(1)} fusion(bf16[2048,1024]{1,0:T(8,128)(2,1)} %all-gather.5.cloned.1.call-done, bf16[1024,256]{1,0:T(8,128)(2,1)S(1)} %copy-done), kind=kOutput, calls=%fused_computation.23 | convolution fusion | flops 1074266112 | bytes 5767168 | tf_op jit(solution)/shard_map/dot_general | solution.py:40
  49.3 0.6 copy.26
  49.9 0.2 copy.34
  50.2 4.4 %convolution_convert_fusion = bf16[2048,256]{1,0:T(8,128)(2,1)} fusion(bf16[2048,1024]{1,0:T(8,128)(2,1)} %all-gather.5.cloned.1.call-done, bf16[1024,256]{1,0:T(8,128)(2,1)S(1)} %copy-done.3), kind=kOutput, calls=%fused_computation.22 | convolution fusion | flops 1074266112 | bytes 5767168 | tf_op jit(solution)/shard_map/dot_general | solution.py:41
  54.6 1.5 copy.27
  56.1 0.2 copy.35
  56.3 1.5 maximum_bitcast_fusion
  57.8 3.4 %copy.28 = bf16[4,16,128,128]{3,2,1,0:T(8,128)(2,1)S(1)} copy(bf16[4,16,128,128]{2,1,3,0:T(8,128)(2,1)} %maximum_bitcast_fusion) | data formatting | bytes 4194304 | tf_op jit(solution)/shard_map/transpose | solution.py:70
  61.3 1.8 broadcast_in_dim.20
  63.1 8.6 %scatter_fusion = bf16[64,128,128]{2,1,0:T(8,128)(2,1)} fusion(bf16[64,128,128]{2,1,0:T(8,128)(2,1)} %broadcast_in_dim.20, s32[64]{0:T(128)S(1)} %fusion.20, bf16[64,128,128]{2,1,0:T(8,128)(2,1)S(1)} %bitcast.55), kind=kCustom, calls=%fused_computation.3 | custom fusion | bytes 6291712 | tf_op jit(solution)/shard_map/scatter | solution.py:71
  71.7 5.4 %all-to-all-start.1 = ((bf16[64,128,128]{2,1,0:T(8,128)(2,1)}), bf16[64,128,128]{2,1,0:T(8,128)(2,1)}, u32[]{:S(2)}, u32[]{:S(2)}) async-start(bf16[64,128,128]{2,1,0:T(8,128)(2,1)} %scatter_fusion), calls=%async_computation.1 | async-start | bytes 4194304 | tf_op jit(solution)/shard_map/all_to_all | solution.py:76
  77.2 0.5 broadcast.249
  77.7 0.7 reduce.3
  78.5 42.5 %all-to-all-done.1 = bf16[64,128,128]{2,1,0:T(8,128)(2,1)} async-done(((bf16[64,128,128]{2,1,0:T(8,128)(2,1)}), bf16[64,128,128]{2,1,0:T(8,128)(2,1)}, u32[]{:S(2)}, u32[]{:S(2)}) %all-to-all-start.1) | async-done | bytes 2097184 | tf_op jit(solution)/shard_map/all_to_all | solution.py:76
  121.0 0.5 broadcast_in_dim.18
  121.5 6.6 %scatter_fusion.1 = bf16[65,128,128]{2,1,0:T(8,128)(2,1)S(1)} fusion(bf16[65,128,128]{2,1,0:T(8,128)(2,1)S(1)} %broadcast_in_dim.18, s32[64]{0:T(128)S(1)} %fusion.21, bf16[64,128,128]{2,1,0:T(8,128)(2,1)} %all-to-all-done.1), kind=kCustom, calls=%fused_computation.4 | custom fusion | bytes 6291712 | tf_op jit(solution)/shard_map/scatter | solution.py:79
  128.1 0.1 slice.28
  128.3 1.3 copy-done.1
  129.6 0.1 copy.33
  129.8 0.2 collective-permute-start
  130.1 3.2 %copy.29 = bf16[64,128,128]{1,2,0:T(8,128)(2,1)S(1)} copy(bf16[64,128,128]{2,1,0:T(8,128)(2,1)} %copy-done.1) | data formatting | bytes 4194304 | tf_op jit(solution)/shard_map/slice | solution.py:80
  133.4 0.1 slice.31
  133.5 0.3 collective-permute-done
  133.8 0.5 pad_maximum_fusion
  134.4 0.7 fusion.2
  135.1 1.3 fusion.9
  136.4 5.4 %fusion.26 = (f32[4,16,128]{2,1,0:T(8,128)S(1)}, f32[4,16,128,256]{3,2,1,0:T(8,128)}) fusion(f32[4,16,128,256]{3,2,1,0:T(8,128)S(1)} %fusion.9, pred[128,256]{1,0:T(8,128)(4,1)S(1)} %iota_compare_fusion), kind=kOutput, calls=%fused_computation.66 | output fusion | flops 12583167 | bytes 16842752 | tf_op jit(solution)/shard_map/sub | solution.py:96
  141.8 4.4 %fusion.14 = bf16[4,16,128,64]{2,3,1,0:T(8,128)(2,1)S(1)} fusion(bf16[4,16,256,128]{2,3,1,0:T(8,128)(2,1)S(1)} %pad_maximum_fusion, f32[4,16,128,256]{3,2,1,0:T(8,128)} %get-tuple-element.111, f32[4,16,128]{2,1,0:T(8,128)S(1)} %get-tuple-element.110), kind=kOutput, calls=%fused_computation.29 | convolution fusion | flops 273154048 | bytes 11567104 | tf_op jit(solution)/shard_map/pbqk,pbkd->pbqd/dot_general | solution.py:98
  146.3 1.7 gather_fusion
  148.0 6.2 %all-to-all-start.2 = ((bf16[64,128,64]{1,2,0:T(8,128)(2,1)}), bf16[64,128,64]{1,2,0:T(8,128)(2,1)S(1)}, u32[]{:S(2)}, u32[]{:S(2)}) async-start(bf16[64,128,64]{1,2,0:T(8,128)(2,1)} %gather_fusion), calls=%async_computation.2 | async-start | bytes 2097152 | tf_op jit(solution)/shard_map/all_to_all | solution.py:105
  154.2 20.9 %all-to-all-done.2 = bf16[64,128,64]{1,2,0:T(8,128)(2,1)S(1)} async-done(((bf16[64,128,64]{1,2,0:T(8,128)(2,1)}), bf16[64,128,64]{1,2,0:T(8,128)(2,1)S(1)}, u32[]{:S(2)}, u32[]{:S(2)}) %all-to-all-start.2) | async-done | bytes 1048608 | tf_op jit(solution)/shard_map/all_to_all | solution.py:105
  175.1 0.8 gather_fusion.1
  175.8 0.7 copy.31
  176.5 1.2 copy.38
  177.8 39.0 %all-gather.7.cloned.1.call-done = bf16[2048,1024]{0,1:T(8,128)(2,1)} async-done(((bf16[2048,256]{0,1:T(8,128)(2,1)}), bf16[2048,1024]{0,1:T(8,128)(2,1)}) %all-gather.7.cloned.1.call-update) | async-done | bytes 4194320 | tf_op jit(solution)/shard_map/all_gather | solution.py:108
  216.8 4.5 %fusion.8 = bf16[2048,256]{1,0:T(8,128)(2,1)} fusion(bf16[2048,1024]{0,1:T(8,128)(2,1)} %all-gather.7.cloned.1.call-done, bf16[1024,256]{1,0:T(8,128)(2,1)S(1)} %copy-done.4, bf16[2048,256]{1,0:T(8,128)(2,1)S(1)} %copy-done.2), kind=kOutput, calls=%fused_computation.21 | convolution fusion | flops 1075314688 | bytes 6815744 | tf_op jit(solution)/shard_map/dot_general | solution.py:109
  (42 shorter events, 0.8 us)
Async XLA Ops:
  6.5 39.2 %copy-start = (bf16[1024,256]{1,0:T(8,128)(2,1)S(1)}, bf16[1024,256]{1,0:T(8,128)(2,1)}, u32[]{:S(2)}) copy-start(bf16[1024,256]{1,0:T(8,128)(2,1)} %param.9) | copy-start | bytes 1572868
  6.5 39.2 %all-gather.5.cloned.1.call-start = ((), (), s32[]{:S(2)}) async-start(), calls=%async_computation.3 | async-start | bytes 5242880 | tf_op jit(solution)/shard_map/all_gather | solution.py:39
  38.7 33.0 %all-to-all-start = ((s32[8,8,1]{1,2,0:T(1,128)}), s32[8,8,1]{1,2,0:T(1,128)S(1)}, u32[]{:S(2)}, u32[]{:S(2)}) async-start(s32[8,8,1]{1,2,0:T(1,128)} %bitcast.4), calls=%async_computation | async-start | bytes 8192 | tf_op jit(solution)/shard_map/all_to_all | solution.py:77
  45.7 4.4 %copy-start.3 = (bf16[1024,256]{1,0:T(8,128)(2,1)S(1)}, bf16[1024,256]{1,0:T(8,128)(2,1)}, u32[]{:S(2)}) copy-start(bf16[1024,256]{1,0:T(8,128)(2,1)} %param.10) | copy-start | bytes 1572868
  71.7 49.2 %all-to-all-start.1 = ((bf16[64,128,128]{2,1,0:T(8,128)(2,1)}), bf16[64,128,128]{2,1,0:T(8,128)(2,1)}, u32[]{:S(2)}, u32[]{:S(2)}) async-start(bf16[64,128,128]{2,1,0:T(8,128)(2,1)} %scatter_fusion), calls=%async_computation.1 | async-start | bytes 4194304 | tf_op jit(solution)/shard_map/all_to_all | solution.py:76
  128.3 1.4 copy-start.1
  129.8 4.1 %collective-permute-start = (bf16[4,128,128]{1,2,0:T(8,128)(2,1)S(1)}, bf16[4,128,128]{1,2,0:T(8,128)(2,1)S(1)}, u32[]{:S(2)}, u32[]{:S(2)}) collective-permute-start(bf16[4,128,128]{1,2,0:T(8,128)(2,1)S(1)} %bitcast.64), channel_id=1, source_target_pairs={{0,4},{4,8},{8,12},{12,16},{16,20},{20,24},{24,28},{28,0},{1,5},{5... | collective-permute-start | bytes 393224 | tf_op jit(solution)/shard_map/ppermute | solution.py:25
  148.0 27.1 %all-to-all-start.2 = ((bf16[64,128,64]{1,2,0:T(8,128)(2,1)}), bf16[64,128,64]{1,2,0:T(8,128)(2,1)S(1)}, u32[]{:S(2)}, u32[]{:S(2)}) async-start(bf16[64,128,64]{1,2,0:T(8,128)(2,1)} %gather_fusion), calls=%async_computation.2 | async-start | bytes 2097152 | tf_op jit(solution)/shard_map/all_to_all | solution.py:105
  154.2 62.6 %all-gather.7.cloned.1.call-start = ((), (), s32[]{:S(2)}) async-start(), calls=%async_computation.4 | async-start | bytes 5242880 | tf_op jit(solution)/shard_map/all_gather | solution.py:108
  154.2 62.6 %copy-start.4 = (bf16[1024,256]{1,0:T(8,128)(2,1)S(1)}, bf16[1024,256]{1,0:T(8,128)(2,1)}, u32[]{:S(2)}) copy-start(bf16[1024,256]{1,0:T(8,128)(2,1)} %param.11) | copy-start | bytes 1572868
  175.8 41.0 %copy-start.2 = (bf16[2048,256]{1,0:T(8,128)(2,1)S(1)}, bf16[2048,256]{1,0:T(8,128)(2,1)}, u32[]{:S(2)}) copy-start(bf16[2048,256]{1,0:T(8,128)(2,1)} %param.7) | copy-start | bytes 3145732
Sparse Core Ops, SparseCore 0:
  8.9 36.3 all-gather.4
  177.9 38.8 all-gather.6
where the time goes:
time: 231 us; the launch traced here: 228 us
  waiting for transfers between devices  103 us (45%)
  local copies, waits for them, and re-layouts  35.4 us (15%)
  blocking collectives  26.2 us (11%)
  starting transfers between devices  18.9 us (8%)
  matrix products  18.2 us (8%)
  between operations  13.7 us (6%)
  other arithmetic  12.1 us (5%)
    all_to_all x1, waiting for transfers between devices, per_device(): lax.all_to_all(outbox, 'seq', split_axis=0, concat_axis=0, tiled=True)  42.5 us
    all_gather x1, waiting for transfers between devices, per_device(): heads_all = lax.all_gather(head_local, 'head', axis=1, tiled=True)  39 us
    all_to_all x1, waiting for transfers between devices, per_device(): lax.all_to_all(replies, 'seq', split_axis=0, concat_axis=0, tiled=True)  20.9 us
    all_gather x1, blocking collectives, carried_in(): everything = lax.all_gather(x, axis)  20.6 us
    scatter x1, local copies, waits for them, and re-layouts, per_device(): jnp.zeros((seq_count * capacity, BLK, 2 * DH), jnp.bfloat16).at[target]  8.65 us
    all_to_all x1, starting transfers between devices, per_device(): lax.all_to_all(outbox_index, 'seq', split_axis=0, concat_axis=0, tiled=True)  7 us
    scatter x1, local copies, waits for them, and re-layouts, per_device(): jnp.zeros((item_count + 1, BLK, 2 * DH), jnp.bfloat16).at[received_index]  6.62 us
    all_to_all x1, starting transfers between devices, per_device(): lax.all_to_all(replies, 'seq', split_axis=0, concat_axis=0, tiled=True)  6.2 us
  transfers between devices with their start and end apart: 6, of which 4 were waited for; matrix products, arithmetic and copies ran while one was open for 15% of the time, Pallas kernels for 0%

commit v1 on v0

v1 whole, which is shorter than its diff:
```python
import functools

import jax
import jax.numpy as jnp
from jax import lax
from jax.experimental import pallas as pl
from jax.experimental.pallas import tpu as pltpu
from jax.sharding import PartitionSpec as P

DH = 64
BLK = 128
HG = 4
CH = 256
MESH = pl.DeviceIdType.MESH


def head_ring():
    g = lax.axis_index("head")
    h1 = g + 1 - 2 * lax.rem(g, 2)
    h2 = g + 2 - 4 * lax.div(g, 2)
    h3 = h1 + 2 - 4 * lax.div(h1, 2)
    return g, h1, h2, h3


def remote(src, dst, send, recv, seq, head):
    return pltpu.make_async_remote_copy(
        src_ref=src, dst_ref=dst, send_sem=send, recv_sem=recv,
        device_id=(seq, head), device_id_type=MESH,
    )


def greet(n, i, g, h1, h2):
    barrier = pltpu.get_barrier_semaphore()

    def say(p, c):
        pl.semaphore_signal(barrier, inc=1, device_id=(lax.rem(i + p, n), g), device_id_type=MESH)
        return c

    lax.fori_loop(1, n, say, 0)
    for h in (h1, h2):
        pl.semaphore_signal(barrier, inc=1, device_id=(i, h), device_id_type=MESH)
    pl.semaphore_wait(barrier, n + 1)


def project_kernel(n, nc, tok, buck, ws, wv, items, ball, g1, g2, g3, ids,
                   s1, r1, s2, r2, s3, r3, sb, rb, sh, rh):
    i = lax.axis_index("seq")
    g, h1, h2, h3 = head_ring()
    greet(n, i, g, h1, h2)

    def over_x(c):
        return remote(tok.at[c], g2.at[c], s2.at[c], r2.at[c], i, h2)

    def over_core(c):
        return remote(tok.at[c], g1.at[c], s1.at[c], r1.at[c], i, h1)

    def onward(c):
        return remote(g2.at[c], g3.at[c], s3.at[c], r3.at[c], i, h1)

    def launch(c, carry):
        over_x(c).start()
        over_core(c).start()
        return carry

    lax.fori_loop(0, nc, launch, 0)
    ids[0, i] = buck[...]

    def bucket_copy(p):
        peer = lax.rem(i + p, n)
        return remote(buck, ids.at[0, i], sb.at[peer], rb.at[i], peer, g)

    def bucket_start(p, carry):
        bucket_copy(p).start()
        return carry

    lax.fori_loop(1, n, bucket_start, 0)

    def bucket_wait(p, carry):
        src = lax.rem(i + n - p, n)
        remote(buck, ids.at[0, src], sb.at[src], rb.at[src], src, g).wait_recv()
        return carry

    lax.fori_loop(1, n, bucket_wait, 0)
    id1 = remote(ids.at[0], ids.at[1], sh.at[0], rh.at[0], i, h1)
    id2 = remote(ids.at[0], ids.at[2], sh.at[1], rh.at[1], i, h2)
    id3 = remote(ids.at[2], ids.at[3], sh.at[2], rh.at[2], i, h1)
    id1.start()
    id2.start()

    def forward(c):
        over_x(c).wait_recv()
        onward(c).start()

    def compute(c):
        over_core(c).wait_recv()
        onward(c).wait_recv()
        shared = jnp.zeros((CH, HG * DH), jnp.float32)
        value = jnp.zeros((CH, HG * DH), jnp.float32)
        for ref, h in ((tok, g), (g1, h1), (g2, h2), (g3, h3)):
            x = ref[c]
            at = pl.ds(pl.multiple_of(h * CH, CH), CH)
            shared += jnp.dot(x, ws[at, :], preferred_element_type=jnp.float32)
            value += jnp.dot(x, wv[at, :], preferred_element_type=jnp.float32)
        shared = shared.astype(jnp.bfloat16)
        value = value.astype(jnp.bfloat16)
        for b in range(CH // BLK):
            for h in range(HG):
                rows, cols = slice(b * BLK, (b + 1) * BLK), slice(h * DH, (h + 1) * DH)
                items[(c * (CH // BLK) + b) * HG + h] = jnp.concatenate(
                    [shared[rows, cols], value[rows, cols]], axis=1)

    forward(0)

    def step(c, carry):
        forward(c)
        compute(c - 1)
        return carry

    lax.fori_loop(1, nc, step, 0)
    id2.wait_recv()
    id3.start()
    compute(nc - 1)
    id1.wait_recv()
    id3.wait_recv()
    ball[...] = ids[...]

    def drain(c, carry):
        over_x(c).wait_send()
        over_core(c).wait_send()
        onward(c).wait_send()
        return carry

    lax.fori_loop(0, nc, drain, 0)

    def bucket_drain(p, carry):
        bucket_copy(p).wait_send()
        return carry

    lax.fori_loop(1, n, bucket_drain, 0)
    id1.wait_send()
    id2.wait_send()
    id3.wait_send()


def attend_kernel(n, cap, nb, idx, items, tok, wo, out, outbox, inbox, tail_out, tail_in, out2, ans,
                  sa, ra, st, rt, sr, rr, s1, r1, s2, r2, s3, r3):
    i = lax.axis_index("seq")
    g, h1, h2, h3 = head_ring()
    slots = n * cap
    at_pred, at_tail, at_target = slots, 2 * slots, 2 * slots + HG
    greet(n, i, g, h1, h2)

    def chunk(o):
        return pl.ds(o * cap, cap)

    def outward(p):
        peer = lax.rem(i + p, n)
        return remote(outbox.at[peer], inbox.at[chunk(i)], sa.at[peer], ra.at[i], peer, g)

    def pack(p, carry):
        peer = lax.rem(i + p, n)
        for k in range(cap):
            outbox[peer, k] = items[idx[peer * cap + k]]
        outward(p).start()
        return carry

    lax.fori_loop(1, n, pack, 0)
    for k in range(cap):
        inbox[i * cap + k] = items[idx[i * cap + k]]
    for h in range(HG):
        inbox[slots + h] = jnp.zeros((BLK, 2 * DH), jnp.bfloat16)

    def arrive(p, carry):
        src = lax.rem(i + n - p, n)
        remote(outbox.at[src], inbox.at[chunk(src)], sa.at[src], ra.at[src], src, g).wait_recv()
        return carry

    lax.fori_loop(1, n, arrive, 0)
    for h in range(HG):
        tail_out[h] = inbox[idx[at_tail + h]]
    tail = remote(tail_out, tail_in, st.at[0], rt.at[0], lax.rem(i + 1, n), g)
    tail.start()
    tail.wait_recv()
    for h in range(HG):
        inbox[slots + h] = tail_in[h]

    lane = lax.broadcasted_iota(jnp.int32, (1, 2 * DH), 1)
    is_key = (lane < DH).astype(jnp.float32)
    row_at = lax.broadcasted_iota(jnp.int32, (BLK, 2 * BLK), 0)
    col_at = lax.broadcasted_iota(jnp.int32, (BLK, 2 * BLK), 1)
    itself = col_at == row_at + BLK

    def attend(j):
        own = inbox[j]
        keys = jnp.concatenate([inbox[idx[at_pred + j]], own], axis=0)
        query = (own.astype(jnp.float32) * (is_key * (DH ** -0.5))).astype(jnp.bfloat16)
        kf = keys.astype(jnp.float32) * is_key
        square = jnp.sum(kf * kf, axis=1, keepdims=True) * (1.0 / DH)
        khat = (kf * lax.rsqrt(square + 1e-6)).astype(jnp.bfloat16)
        scores = lax.dot_general(query, khat, (((1,), (1,)), ((), ())),
                                 preferred_element_type=jnp.float32)
        scores = jnp.where(itself, jnp.float32(-100000.0), scores)
        expo = jnp.exp(scores - jnp.max(scores, axis=1, keepdims=True))
        weights = (expo * (1.0 / jnp.sum(expo, axis=1, keepdims=True))).astype(jnp.bfloat16)
        mixed = jnp.dot(weights, keys, preferred_element_type=jnp.float32).astype(jnp.bfloat16)
        return jnp.concatenate([mixed[: BLK // 2, DH:], mixed[BLK // 2:, DH:]], axis=1)

    def reply(p):
        peer = lax.rem(i + p, n)
        return remote(out2.at[peer], ans.at[0, chunk(i)], sr.at[peer], rr.at[i], peer, g)

    def relay1(o):
        return remote(ans.at[0, chunk(o)], ans.at[1, chunk(o)], s1.at[o], r1.at[o], i, h1)

    def relay2(o):
        return remote(ans.at[0, chunk(o)], ans.at[2, chunk(o)], s2.at[o], r2.at[o], i, h2)

    def relay3(o):
        return remote(ans.at[2, chunk(o)], ans.at[3, chunk(o)], s3.at[o], r3.at[o], i, h1)

    for k in range(cap):
        ans[0, i * cap + k] = attend(i * cap + k)
    relay2(i).start()
    relay1(i).start()

    def answer(p, carry):
        peer = lax.rem(i + p, n)
        for k in range(cap):
            out2[peer, k] = attend(peer * cap + k)
        reply(p).start()
        return carry

    lax.fori_loop(1, n, answer, 0)

    def relay(p, carry):
        src = lax.rem(i + n - p, n)
        remote(out2.at[src], ans.at[0, chunk(src)], sr.at[src], rr.at[src], src, g).wait_recv()
        relay2(src).start()
        relay1(src).start()
        before = lax.rem(i + n - p + 1, n)
        relay2(before).wait_recv()
        relay3(before).start()
        return carry

    lax.fori_loop(1, n, relay, 0)
    last = lax.rem(i + 1, n)
    relay2(last).wait_recv()
    relay3(last).start()

    def settle(o, carry):
        relay1(o).wait_recv()
        relay3(o).wait_recv()
        return carry

    lax.fori_loop(0, n, settle, 0)

    group = 4

    def finish(q, carry):
        total = jnp.zeros((group * BLK, wo.shape[1]), jnp.float32)
        for r, h in enumerate((g, h1, h2, h3)):
            rows = []
            for b in range(group):
                at = at_target + (r * nb + q * group + b) * HG
                parts = [ans[r, idx[at + k]] for k in range(HG)]
                rows.append(jnp.concatenate([x[:, :DH] for x in parts], axis=1))
                rows.append(jnp.concatenate([x[:, DH:] for x in parts], axis=1))
            total += jnp.dot(jnp.concatenate(rows, axis=0),
                             wo[pl.ds(pl.multiple_of(h * HG * DH, HG * DH), HG * DH), :],
                             preferred_element_type=jnp.float32)
        at = pl.ds(q * group, group)
        base = tok[at].reshape(group * BLK, -1).astype(jnp.float32)
        out[at] = (base + total).astype(jnp.bfloat16).reshape(group, BLK, -1)
        return carry

    lax.fori_loop(0, nb // group, finish, 0)

    def drain(p, carry):
        outward(p).wait_send()
        reply(p).wait_send()
        return carry

    lax.fori_loop(1, n, drain, 0)
    tail.wait_send()

    def drain_relays(o, carry):
        relay1(o).wait_send()
        relay2(o).wait_send()
        relay3(o).wait_send()
        return carry

    lax.fori_loop(0, n, drain_relays, 0)


def index_tables(ball, n, nb, cap):
    i = lax.axis_index("seq")
    blocks, slots = n * nb, n * cap
    key = ball[..., :HG].reshape(HG, blocks, HG) * blocks + jnp.arange(blocks, dtype=jnp.int32)[None, :, None]
    key = jnp.transpose(key, (0, 2, 1))
    position = jnp.sum((key[:, :, None, :] < key[:, :, :, None]).astype(jnp.int32), axis=3)
    position = jnp.transpose(position, (0, 2, 1)).reshape(HG, n, nb * HG)
    count = nb * HG
    item = jnp.arange(count, dtype=jnp.int32)
    owner, within = position // nb, position % nb
    same = owner[..., :, None] == owner[..., None, :]
    slot = jnp.sum((same & (item[None, :] < item[:, None])).astype(jnp.int32), axis=3)
    target = lax.dynamic_index_in_dim(owner * cap + slot, i, 1, keepdims=False)
    slot_ids = jnp.arange(slots, dtype=jnp.int32)
    inverse = jnp.sum(jnp.where(target[0][None, :] == slot_ids[:, None], item[None, :], 0), axis=1)
    place = (jnp.arange(n, dtype=jnp.int32)[:, None] * cap + slot[0]).reshape(-1)
    mine = (owner[0] == i).reshape(-1)
    grid = ((item % HG)[None, :] * nb + within[0]).reshape(-1)
    grid_of = jnp.sum(jnp.where(mine & (place == slot_ids[:, None]), grid, 0), axis=1)
    slot_of = jnp.sum(jnp.where(mine & (grid == item[:, None]), place, 0), axis=1)
    inside = jnp.sum(jnp.where(item[None, :] == grid_of[:, None] - 1, slot_of[None, :], 0), axis=1)
    before = jnp.where(grid_of % nb == 0, slots + grid_of // nb, inside)
    tails = slot_of.reshape(HG, nb)[:, nb - 1]
    return jnp.concatenate([inverse, before, tails, target.reshape(-1)]).astype(jnp.int32)


def per_device(tokens, buckets, w_shared, w_value, w_output):
    n = lax.axis_size("seq")
    nb = buckets.shape[0]
    rows, width = tokens.shape
    cap = max(1, nb * HG // n)
    nc = rows // CH
    vmem = pl.BlockSpec(memory_space=pltpu.VMEM)
    dma = lambda k: pltpu.SemaphoreType.DMA((k,))
    bf = jnp.bfloat16
    padded = jnp.pad(buckets, ((0, 0), (0, 128 - HG)))
    items, ball = pl.pallas_call(
        functools.partial(project_kernel, n, nc),
        out_shape=(jax.ShapeDtypeStruct((nb * HG, BLK, 2 * DH), bf),
                   jax.ShapeDtypeStruct((HG, n, nb, 128), jnp.int32)),
        in_specs=[vmem] * 4,
        out_specs=(vmem, vmem),
        scratch_shapes=[pltpu.VMEM((nc, CH, width), bf)] * 3
        + [pltpu.VMEM((HG, n, nb, 128), jnp.int32)]
        + [dma(nc)] * 6 + [dma(n), dma(n), dma(3), dma(3)],
        compiler_params=pltpu.CompilerParams(collective_id=0, has_side_effects=True,
                                             vmem_limit_bytes=40 << 20),
    )(tokens.reshape(nc, CH, width), padded, w_shared, w_value)
    idx = index_tables(ball, n, nb, cap)
    slots = n * cap
    out = pl.pallas_call(
        functools.partial(attend_kernel, n, cap, nb),
        out_shape=jax.ShapeDtypeStruct((nb, BLK, width), bf),
        in_specs=[pl.BlockSpec(memory_space=pltpu.SMEM)] + [vmem] * 3,
        out_specs=vmem,
        scratch_shapes=[
            pltpu.VMEM((n, cap, BLK, 2 * DH), bf),
            pltpu.VMEM((slots + HG, BLK, 2 * DH), bf),
            pltpu.VMEM((HG, BLK, 2 * DH), bf),
            pltpu.VMEM((HG, BLK, 2 * DH), bf),
            pltpu.VMEM((n, cap, BLK // 2, 2 * DH), bf),
            pltpu.VMEM((HG, slots, BLK // 2, 2 * DH), bf),
        ] + [dma(n), dma(n), dma(1), dma(1), dma(n), dma(n)] + [dma(n)] * 6,
        compiler_params=pltpu.CompilerParams(collective_id=1, has_side_effects=True,
                                             vmem_limit_bytes=40 << 20),
    )(idx, items, tokens.reshape(nb, BLK, width), w_output)
    return out.reshape(rows, width)


def solution(mesh):
    return jax.shard_map(
        per_device,
        mesh=mesh,
        in_specs=(
            P("seq", "head"),
            P("seq", "head"),
            P(None, "head"),
            P(None, "head"),
            P(None, "head"),
        ),
        out_specs=P("seq", "head"),
        check_vma=False,
    )
```

time: 231 us -> 145 us (0.63)
  Pallas kernels: 0 us -> 133 us
  waiting for transfers between devices: 103 us -> 0 us
  local copies, waits for them, and re-layouts: 35.4 us -> 7.84 us
  blocking collectives: 26.2 us -> 0 us
  starting transfers between devices: 18.9 us -> 0 us
  matrix products: 18.2 us -> 0 us
  between operations: 13.7 us -> 0.13 us
  other arithmetic: 12.1 us -> 2.89 us
    pallas_call x0 -> x2, Pallas kernels: none -> 133 us  [the longest x1 104 us: per_device(): pl.pallas_call(functools.partial(attend_kernel, n, cap, nb), out_shape=ja...]
    all_to_all x3 -> x0, waiting for transfers between devices: 63.4 us -> none  [the longest x1 42.5 us: per_device(): lax.all_to_all(outbox, 'seq', split_axis=0, concat_axis=0, tiled=True)]
    all_gather x2 -> x0, waiting for transfers between devices: 39 us -> none  [the longest x1 39 us: per_device(): heads_all = lax.all_gather(head_local, 'head', axis=1, tiled=True)]
    all_gather x1 -> x0, blocking collectives: 20.6 us -> none  [carried_in(): everything = lax.all_gather(x, axis)]
    all_to_all x3 -> x0, starting transfers between devices: 18.6 us -> none  [the longest x1 7 us: per_device(): lax.all_to_all(outbox_index, 'seq', split_axis=0, concat_axis=0, tiled=True)]
    dot_general x5 -> x0, matrix products: 18.2 us -> none  [the longest x1 4.54 us: per_device(): jnp.dot(heads_all, w_output, preferred_element_type=jnp.float32)]
    scatter x3 -> x0, local copies, waits for them, and re-layouts: 16 us -> none  [the longest x1 8.65 us: per_device(): jnp.zeros((seq_count * capacity, BLK, 2 * DH), jnp.bfloat16).at[target]]
    psum x1 -> x0, blocking collectives: 5.62 us -> none  [per_device(): total = lax.psum(counts, 'seq')]
  transfers between devices with their start and end apart: 6 -> 0, of which waited for: 4 -> 0; matrix products, arithmetic and copies ran while one was open for 15% -> 0% of each run, Pallas kernels for 0% -> 0%
where the time goes in v1:
time: 145 us; the launch traced here: 144 us
  Pallas kernels  133 us (92%)
  local copies, waits for them, and re-layouts  7.84 us (5%)
  other arithmetic  2.89 us (2%)
    pallas_call x1, Pallas kernels, per_device(): pl.pallas_call(functools.partial(attend_kernel, n, cap, nb), out_shape=ja...  104 us
    pallas_call x1, Pallas kernels, per_device(): pl.pallas_call(functools.partial(project_kernel, n, nc), out_shape=(jax.S...  28.9 us
    unnamed x12, local copies, waits for them, and re-layouts  6.08 us

profile of v1, /device:TPU:29, one launch (start us, length us, event | category | flops | bytes accessed | tf_op | source)
XLA Modules:
  0.0 143.7 jit_solution(4959924967923403900)
XLA Ops:
  0.0 0.1 add.98
  0.1 0.1 add.93
  0.2 0.1 add.94
  0.2 0.8 copy.12
  1.0 0.0 copy-start
  1.0 1.2 copy-done
  2.3 0.0 copy-start.3
  2.3 1.0 copy-done.3
  3.3 0.0 copy-start.4
  3.3 1.0 copy-done.4
  4.3 0.0 copy-start.1
  4.3 28.9 %shard_map.55 = (bf16[64,128,128]{2,1,0:T(8,128)(2,1)S(1)}, s32[4,8,16,128]{3,2,1,0:T(8,128)S(1)}) custom-call(bf16[8,256,256]{2,1,0:T(8,128)(2,1)S(1)} %bitcast.9, s32[16,128]{1,0:T(8,128)S(1)} %pad.4.buck, bf16[1024,256]{1,0:T(8,128)(2,1)S(1)} %copy-done.3, bf16[1024,256]{1,0:T(8,128)(2,1)S(1)} %copy-done.4), custom_call_target="tpu_custom_call" | custom-call | tf_op jit(solution)/shard_map/pallas_call | solution.py:331
  33.3 0.1 copy.13
  33.4 0.7 convert_reduce_fusion.1
  34.1 0.2 copy.15
  34.3 0.2 reshape.151
  34.5 0.1 squeeze.13
  34.6 0.1 eq.91
  34.6 0.9 convert_reduce_fusion
  35.6 0.5 broadcast.158
  36.1 0.7 fusion.4
  36.8 0.1 squeeze.12
  36.8 0.2 select_reduce_fusion.1
  37.0 0.1 reshape.153
  37.1 0.1 select_reduce_fusion.3
  37.2 0.2 select_reduce_fusion.2
  37.4 0.1 reshape.152
  37.5 0.2 slice_reduce_fusion
  37.7 0.1 pad_add_fusion.idx
  37.8 0.0 copy-done.1
  37.8 0.0 copy-start.2
  37.8 1.0 copy-done.2
  38.8 103.9 %shard_map.56 = bf16[16,128,256]{2,1,0:T(8,128)(2,1)S(1)} custom-call(s32[388]{0:T(512)S(1)} %pad_add_fusion.idx, bf16[64,128,128]{2,1,0:T(8,128)(2,1)S(1)} %get-tuple-element.8.items, bf16[16,128,256]{2,1,0:T(8,128)(2,1)S(1)} %bitcast.10, bf16[1024,256]{1,0:T(8,128)(2,1)S(1)} %copy-done.2), custom_call_target="tpu_custom_call" | custom-call | tf_op jit(solution)/shard_map/pallas_call | solution.py:345
  142.8 1.0 copy.17
  (17 shorter events, 0.1 us)
Async XLA Ops:
  1.0 1.2 copy-start
  2.3 1.0 copy-start.3
  3.3 1.0 copy-start.4
  4.3 33.4 %copy-start.1 = (bf16[2048,256]{1,0:T(8,128)(2,1)S(1)}, bf16[2048,256]{1,0:T(8,128)(2,1)}, u32[]{:S(2)}) copy-start(bf16[2048,256]{1,0:T(8,128)(2,1)} %param.5) | copy-start | bytes 3145732
  37.8 1.0 copy-start.2

commit v2 on v1

--- a/solution.py
+++ b/solution.py
@@ -42,10 +42,14 @@
     pl.semaphore_wait(barrier, n + 1)
 
 
-def project_kernel(n, nc, tok, buck, ws, wv, items, ball, g1, g2, g3, ids,
-                   s1, r1, s2, r2, s3, r3, sb, rb, sh, rh):
+def project_kernel(n, nc, tok, buck, ws_hbm, wv_hbm, items_s, items_v, ball, own, ws, wv, g1, g2, g3, ids,
+                   local, s1, r1, s2, r2, s3, r3, sb, rb, sh, rh):
     i = lax.axis_index("seq")
     g, h1, h2, h3 = head_ring()
+    loads = [pltpu.make_async_copy(src, dst, local.at[k])
+             for k, (src, dst) in enumerate(((tok, own), (ws_hbm, ws), (wv_hbm, wv)))]
+    for load in loads:
+        load.start()
     greet(n, i, g, h1, h2)
 
     def over_x(c):
@@ -96,19 +100,21 @@
         onward(c).wait_recv()
         shared = jnp.zeros((CH, HG * DH), jnp.float32)
         value = jnp.zeros((CH, HG * DH), jnp.float32)
-        for ref, h in ((tok, g), (g1, h1), (g2, h2), (g3, h3)):
+        for ref, h in ((own, g), (g1, h1), (g2, h2), (g3, h3)):
             x = ref[c]
             at = pl.ds(pl.multiple_of(h * CH, CH), CH)
             shared += jnp.dot(x, ws[at, :], preferred_element_type=jnp.float32)
             value += jnp.dot(x, wv[at, :], preferred_element_type=jnp.float32)
-        shared = shared.astype(jnp.bfloat16)
-        value = value.astype(jnp.bfloat16)
-        for b in range(CH // BLK):
-            for h in range(HG):
-                rows, cols = slice(b * BLK, (b + 1) * BLK), slice(h * DH, (h + 1) * DH)
-                items[(c * (CH // BLK) + b) * HG + h] = jnp.concatenate(
-                    [shared[rows, cols], value[rows, cols]], axis=1)
-
+        for full, dst in ((shared.astype(jnp.bfloat16), items_s), (value.astype(jnp.bfloat16), items_v)):
+            for b in range(CH // BLK):
+                for h in range(HG):
+                    cols = slice(h * DH, (h + 1) * DH)
+                    dst[(c * (CH // BLK) + b) * HG + h] = jnp.concatenate(
+                        [full[b * BLK: b * BLK + BLK // 2, cols],
+                         full[b * BLK + BLK // 2: (b + 1) * BLK, cols]], axis=1)
+
+    for load in loads:
+        load.wait()
     forward(0)
 
     def step(c, carry):
@@ -142,8 +148,9 @@
     id3.wait_send()
 
 
-def attend_kernel(n, cap, nb, idx, items, tok, wo, out, outbox, inbox, tail_out, tail_in, out2, ans,
-                  sa, ra, st, rt, sr, rr, s1, r1, s2, r2, s3, r3):
+def attend_kernel(n, cap, nb, idx, items_s, items_v, tok, wo, out, s_out, v_out, s_in, v_in,
+                  ts_out, ts_in, tv_out, tv_in, qbuf, kbuf, vbuf, wbuf, out2, ans,
+                  sa, ra, sv, rv, st, rt, sr, rr, s1, r1, s2, r2, s3, r3):
     i = lax.axis_index("seq")
     g, h1, h2, h3 = head_ring()
     slots = n * cap
@@ -153,57 +160,115 @@
     def chunk(o):
         return pl.ds(o * cap, cap)
 
-    def outward(p):
-        peer = lax.rem(i + p, n)
-        return remote(outbox.at[peer], inbox.at[chunk(i)], sa.at[peer], ra.at[i], peer, g)
-
-    def pack(p, carry):
-        peer = lax.rem(i + p, n)
-        for k in range(cap):
-            outbox[peer, k] = items[idx[peer * cap + k]]
-        outward(p).start()
-        return carry
-
-    lax.fori_loop(1, n, pack, 0)
+    def send_s(p):
+        peer = lax.rem(i + p, n)
+        return remote(s_out.at[peer], s_in.at[chunk(i)], sa.at[peer], ra.at[i], peer, g)
+
+    def send_v(p):
+        peer = lax.rem(i + p, n)
+        return remote(v_out.at[peer], v_in.at[chunk(i)], sv.at[peer], rv.at[i], peer, g)
+
+    def pack_s(p, carry):
+        peer = lax.rem(i + p, n)
+        for k in range(cap):
+            s_out[peer, k] = items_s[idx[peer * cap + k]]
+        send_s(p).start()
+        return carry
+
+    lax.fori_loop(1, n, pack_s, 0)
+
+    def pack_v(p, carry):
+        peer = lax.rem(i + p, n)
+        for k in range(cap):
+            v_out[peer, k] = items_v[idx[peer * cap + k]]
+        return carry
+
+    lax.fori_loop(1, n, pack_v, 0)
     for k in range(cap):
-        inbox[i * cap + k] = items[idx[i * cap + k]]
+        s_in[i * cap + k] = items_s[idx[i * cap + k]]
+        v_in[i * cap + k] = items_v[idx[i * cap + k]]
+
+    low = lax.broadcasted_iota(jnp.int32, (BLK // 2, 2 * DH), 1) < DH
+    query_scale = jnp.where(lax.broadcasted_iota(jnp.int32, (1, 2 * DH), 1) < DH,
+                            jnp.float32(DH ** -0.5), jnp.float32(0.0))
+
+    def unfold(x):
+        x = x.astype(jnp.float32)
+        turned = pltpu.roll(x, DH, 1)
+        return jnp.concatenate([jnp.where(low, x, turned), jnp.where(low, turned, x)], axis=0)
+
+    def khat_of(x):
+        square = jnp.sum(x * x, axis=1, keepdims=True) * (0.5 / DH)
+        return (x * lax.rsqrt(square + 1e-6)).astype(jnp.bfloat16)
+
+    def ready_s(o):
+        for k in range(cap):
+            j = o * cap + k
+            x = unfold(s_in[j])
+            qbuf[j] = (x * query_scale).astype(jnp.bfloat16)
+            kbuf[j] = khat_of(x)
+
+    def ready_v(o):
+        for k in range(cap):
+            j = o * cap + k
+            vbuf[j] = unfold(v_in[j]).astype(jnp.bfloat16)
+
+    ready_s(i)
+
+    def arrive_s(p, carry):
+        src = lax.rem(i + n - p, n)
+        remote(s_out.at[src], s_in.at[chunk(src)], sa.at[src], ra.at[src], src, g).wait_recv()
+        send_v(p).start()
+        ready_s(src)
+        return carry
+
+    lax.fori_loop(1, n, arrive_s, 0)
     for h in range(HG):
-        inbox[slots + h] = jnp.zeros((BLK, 2 * DH), jnp.bfloat16)
-
-    def arrive(p, carry):
-        src = lax.rem(i + n - p, n)
-        remote(outbox.at[src], inbox.at[chunk(src)], sa.at[src], ra.at[src], src, g).wait_recv()
-        return carry
-
-    lax.fori_loop(1, n, arrive, 0)
+        ts_out[h] = s_in[idx[at_tail + h]]
+    following = lax.rem(i + 1, n)
+    tail_s = remote(ts_out, ts_in, st.at[0], rt.at[0], following, g)
+    tail_s.start()
+    ready_v(i)
+    tail_s.wait_recv()
     for h in range(HG):
-        tail_out[h] = inbox[idx[at_tail + h]]
-    tail = remote(tail_out, tail_in, st.at[0], rt.at[0], lax.rem(i + 1, n), g)
-    tail.start()
-    tail.wait_recv()
-    for h in range(HG):
-        inbox[slots + h] = tail_in[h]
-
-    lane = lax.broadcasted_iota(jnp.int32, (1, 2 * DH), 1)
-    is_key = (lane < DH).astype(jnp.float32)
+        kbuf[slots + h] = khat_of(unfold(ts_in[h]))
+
     row_at = lax.broadcasted_iota(jnp.int32, (BLK, 2 * BLK), 0)
     col_at = lax.broadcasted_iota(jnp.int32, (BLK, 2 * BLK), 1)
     itself = col_at == row_at + BLK
 
+    def weigh(o, carry):
+        for k in range(cap):
+            j = o * cap + k
+            keys = jnp.concatenate([kbuf[idx[at_pred + j]], kbuf[j]], axis=0)
+            scores = lax.dot_general(qbuf[j], keys, (((1,), (1,)), ((), ())),
+                                     preferred_element_type=jnp.float32)
+            scores = jnp.where(itself, jnp.float32(-100000.0), scores)
+            expo = jnp.exp(scores - jnp.max(scores, axis=1, keepdims=True))
+            wbuf[j] = (expo * (1.0 / jnp.sum(expo, axis=1, keepdims=True))).astype(jnp.bfloat16)
+        return carry
+
+    lax.fori_loop(0, n, weigh, 0)
+
+    def arrive_v(p, carry):
+        src = lax.rem(i + n - p, n)
+        remote(v_out.at[src], v_in.at[chunk(src)], sv.at[src], rv.at[src], src, g).wait_recv()
+        ready_v(src)
+        return carry
+
+    lax.fori_loop(1, n, arrive_v, 0)
+    for h in range(HG):
+        tv_out[h] = v_in[idx[at_tail + h]]
+    tail_v = remote(tv_out, tv_in, st.at[1], rt.at[1], following, g)
+    tail_v.start()
+    tail_v.wait_recv()
+    for h in range(HG):
+        vbuf[slots + h] = unfold(tv_in[h]).astype(jnp.bfloat16)
+
     def attend(j):
-        own = inbox[j]
-        keys = jnp.concatenate([inbox[idx[at_pred + j]], own], axis=0)
-        query = (own.astype(jnp.float32) * (is_key * (DH ** -0.5))).astype(jnp.bfloat16)
-        kf = keys.astype(jnp.float32) * is_key
-        square = jnp.sum(kf * kf, axis=1, keepdims=True) * (1.0 / DH)
-        khat = (kf * lax.rsqrt(square + 1e-6)).astype(jnp.bfloat16)
-        scores = lax.dot_general(query, khat, (((1,), (1,)), ((), ())),
-                                 preferred_element_type=jnp.float32)
-        scores = jnp.where(itself, jnp.float32(-100000.0), scores)
-        expo = jnp.exp(scores - jnp.max(scores, axis=1, keepdims=True))
-        weights = (expo * (1.0 / jnp.sum(expo, axis=1, keepdims=True))).astype(jnp.bfloat16)
-        mixed = jnp.dot(weights, keys, preferred_element_type=jnp.float32).astype(jnp.bfloat16)
-        return jnp.concatenate([mixed[: BLK // 2, DH:], mixed[BLK // 2:, DH:]], axis=1)
+        values = jnp.concatenate([vbuf[idx[at_pred + j]], vbuf[j]], axis=0)
+        mixed = jnp.dot(wbuf[j], values, preferred_element_type=jnp.float32)
+        return jnp.where(low, mixed[: BLK // 2], mixed[BLK // 2:]).astype(jnp.bfloat16)
 
     def reply(p):
         peer = lax.rem(i + p, n)
@@ -276,12 +341,14 @@
     lax.fori_loop(0, nb // group, finish, 0)
 
     def drain(p, carry):
-        outward(p).wait_send()
+        send_s(p).wait_send()
+        send_v(p).wait_send()
         reply(p).wait_send()
         return carry
 
     lax.fori_loop(1, n, drain, 0)
-    tail.wait_send()
+    tail_s.wait_send()
+    tail_v.wait_send()
 
     def drain_relays(o, carry):
         relay1(o).wait_send()
@@ -328,15 +395,19 @@
     dma = lambda k: pltpu.SemaphoreType.DMA((k,))
     bf = jnp.bfloat16
     padded = jnp.pad(buckets, ((0, 0), (0, 128 - HG)))
-    items, ball = pl.pallas_call(
+    hbm = pl.BlockSpec(memory_space=pl.ANY)
+    half = (BLK // 2, 2 * DH)
+    items_s, items_v, ball = pl.pallas_call(
         functools.partial(project_kernel, n, nc),
-        out_shape=(jax.ShapeDtypeStruct((nb * HG, BLK, 2 * DH), bf),
+        out_shape=(jax.ShapeDtypeStruct((nb * HG,) + half, bf),
+                   jax.ShapeDtypeStruct((nb * HG,) + half, bf),
                    jax.ShapeDtypeStruct((HG, n, nb, 128), jnp.int32)),
-        in_specs=[vmem] * 4,
-        out_specs=(vmem, vmem),
-        scratch_shapes=[pltpu.VMEM((nc, CH, width), bf)] * 3
+        in_specs=[hbm, vmem, hbm, hbm],
+        out_specs=(vmem, vmem, vmem),
+        scratch_shapes=[pltpu.VMEM((nc, CH, width), bf), pltpu.VMEM(w_shared.shape, bf), pltpu.VMEM(w_value.shape, bf)]
+        + [pltpu.VMEM((nc, CH, width), bf)] * 3
         + [pltpu.VMEM((HG, n, nb, 128), jnp.int32)]
-        + [dma(nc)] * 6 + [dma(n), dma(n), dma(3), dma(3)],
+        + [dma(3)] + [dma(nc)] * 6 + [dma(n), dma(n), dma(3), dma(3)],
         compiler_params=pltpu.CompilerParams(collective_id=0, has_side_effects=True,
                                              vmem_limit_bytes=40 << 20),
     )(tokens.reshape(nc, CH, width), padded, w_shared, w_value)
@@ -345,19 +416,19 @@
     out = pl.pallas_call(
         functools.partial(attend_kernel, n, cap, nb),
         out_shape=jax.ShapeDtypeStruct((nb, BLK, width), bf),
-        in_specs=[pl.BlockSpec(memory_space=pltpu.SMEM)] + [vmem] * 3,
+        in_specs=[pl.BlockSpec(memory_space=pltpu.SMEM)] + [vmem] * 4,
         out_specs=vmem,
-        scratch_shapes=[
-            pltpu.VMEM((n, cap, BLK, 2 * DH), bf),
-            pltpu.VMEM((slots + HG, BLK, 2 * DH), bf),
-            pltpu.VMEM((HG, BLK, 2 * DH), bf),
-            pltpu.VMEM((HG, BLK, 2 * DH), bf),
-            pltpu.VMEM((n, cap, BLK // 2, 2 * DH), bf),
-            pltpu.VMEM((HG, slots, BLK // 2, 2 * DH), bf),
-        ] + [dma(n), dma(n), dma(1), dma(1), dma(n), dma(n)] + [dma(n)] * 6,
+        scratch_shapes=[pltpu.VMEM((n, cap) + half, bf)] * 2
+        + [pltpu.VMEM((slots,) + half, bf)] * 2
+        + [pltpu.VMEM((HG,) + half, bf)] * 4
+        + [pltpu.VMEM((slots, BLK, 2 * DH), bf)]
+        + [pltpu.VMEM((slots + HG, BLK, 2 * DH), bf)] * 2
+        + [pltpu.VMEM((slots, BLK, 2 * BLK), bf)]
+        + [pltpu.VMEM((n, cap) + half, bf), pltpu.VMEM((HG, slots) + half, bf)]
+        + [dma(n)] * 4 + [dma(2)] * 2 + [dma(n)] * 8,
         compiler_params=pltpu.CompilerParams(collective_id=1, has_side_effects=True,
-                                             vmem_limit_bytes=40 << 20),
-    )(idx, items, tokens.reshape(nb, BLK, width), w_output)
+                                             vmem_limit_bytes=48 << 20),
+    )(idx, items_s, items_v, tokens.reshape(nb, BLK, width), w_output)
     return out.reshape(rows, width)
 
 

time: 145 us -> 140 us (0.966)
  Pallas kernels: 133 us -> 129 us
    pallas_call x1, Pallas kernels: 104 us -> 99.4 us  [per_device(): pl.pallas_call(functools.partial(attend_kernel, n, cap, nb), out_shape=ja...]
    unnamed x12 -> x14, local copies, waits for them, and re-layouts: 6.08 us -> 6.02 us
where the time goes in v2:
time: 140 us; the launch traced here: 139 us
  Pallas kernels  129 us (92%)
  local copies, waits for them, and re-layouts  7.77 us (6%)
  other arithmetic  2.89 us (2%)
    pallas_call x1, Pallas kernels, per_device(): pl.pallas_call(functools.partial(attend_kernel, n, cap, nb), out_shape=ja...  99.4 us
    pallas_call x1, Pallas kernels, per_device(): pl.pallas_call(functools.partial(project_kernel, n, nc), out_shape=(jax.S...  29.2 us
    unnamed x14, local copies, waits for them, and re-layouts  6.02 us

profile of v2, /device:TPU:29, one launch (start us, length us, event | category | flops | bytes accessed | tf_op | source)
XLA Modules:
  0.0 139.3 jit_solution(10679048906229749571)
XLA Ops:
  0.0 0.1 add.98
  0.1 0.1 add.93
  0.2 0.0 copy-start.5
  0.2 0.1 add.94
  0.2 0.6 copy-done.5
  0.8 0.1 copy.12
  1.0 0.0 copy-start
  1.0 1.2 copy-done
  2.2 0.0 copy-start.3
  2.2 1.0 copy-done.3
  3.2 0.0 copy-start.4
  3.2 1.0 copy-done.4
  4.3 29.2 %shard_map.55 = (bf16[64,64,128]{2,1,0:T(8,128)(2,1)S(1)}, bf16[64,64,128]{2,1,0:T(8,128)(2,1)S(1)}, s32[4,8,16,128]{3,2,1,0:T(8,128)S(1)}) custom-call(bf16[8,256,256]{2,1,0:T(8,128)(2,1)S(1)} %bitcast.9, s32[16,128]{1,0:T(8,128)S(1)} %pad.4.buck, bf16[1024,256]{1,0:T(8,128)(2,1)S(1)} %copy-done.3, bf16[1024,256]{1,0:T(8,128)(2,1)S(1)} %copy-done.4), custom_call_target="tpu_custom_call" | custom-call | tf_op jit(solution)/shard_map/pallas_call | solution.py:400
  33.4 0.0 copy-start.1
  33.5 0.1 copy.13
  33.6 0.7 convert_reduce_fusion.1
  34.3 0.2 copy.15
  34.4 0.2 reshape.151
  34.7 0.1 squeeze.13
  34.7 0.1 eq.91
  34.8 0.9 convert_reduce_fusion
  35.8 0.5 broadcast.158
  36.3 0.7 fusion.4
  37.0 0.1 squeeze.12
  37.0 0.2 select_reduce_fusion.1
  37.2 0.1 reshape.153
  37.3 0.1 select_reduce_fusion.3
  37.4 0.2 select_reduce_fusion.2
  37.6 0.1 reshape.152
  37.7 0.2 slice_reduce_fusion
  37.9 0.1 pad_add_fusion.idx
  37.9 0.0 copy-done.1
  37.9 0.0 copy-start.2
  37.9 1.0 copy-done.2
  39.0 99.4 %shard_map.56 = bf16[16,128,256]{2,1,0:T(8,128)(2,1)S(1)} custom-call(s32[388]{0:T(512)S(1)} %pad_add_fusion.idx, bf16[64,64,128]{2,1,0:T(8,128)(2,1)S(1)} %get-tuple-element.9.items_s, bf16[64,64,128]{2,1,0:T(8,128)(2,1)S(1)} %get-tuple-element.10.items_v, bf16[16,128,256]{2,1,0:T(8,128)(2,1)S(1)} %bitcast.10, bf16[1024,256]{1,0:T(8,128)(2,1)S(1)} %copy-done.2), custom_call_target="tpu_custom_call" | custom-call | tf_op jit(solution)/shard_map/pallas_call | solution.py:416
  138.4 1.0 copy.17
  (17 shorter events, 0.1 us)
Async XLA Ops:
  0.2 0.7 copy-start.5
  1.0 1.2 copy-start
  2.2 1.0 copy-start.3
  3.2 1.0 copy-start.4
  33.4 4.5 %copy-start.1 = (bf16[2048,256]{1,0:T(8,128)(2,1)S(1)}, bf16[2048,256]{1,0:T(8,128)(2,1)}, u32[]{:S(2)}) copy-start(bf16[2048,256]{1,0:T(8,128)(2,1)} %param.5) | copy-start | bytes 3145732
  37.9 1.0 copy-start.2

commit v3 on v2

--- a/solution.py
+++ b/solution.py
@@ -288,29 +288,47 @@
     relay2(i).start()
     relay1(i).start()
 
-    def answer(p, carry):
+    def stride(t):
+        return n // 2 + lax.div(t + 1, 2) * (1 - 2 * lax.rem(t, 2))
+
+    def answer(t):
+        p = stride(t)
         peer = lax.rem(i + p, n)
         for k in range(cap):
             out2[peer, k] = attend(peer * cap + k)
         reply(p).start()
-        return carry
-
-    lax.fori_loop(1, n, answer, 0)
-
-    def relay(p, carry):
-        src = lax.rem(i + n - p, n)
+
+    def relay(t):
+        src = lax.rem(i + n - stride(t), n)
         remote(out2.at[src], ans.at[0, chunk(src)], sr.at[src], rr.at[src], src, g).wait_recv()
         relay2(src).start()
         relay1(src).start()
-        before = lax.rem(i + n - p + 1, n)
-        relay2(before).wait_recv()
-        relay3(before).start()
-        return carry
-
-    lax.fori_loop(1, n, relay, 0)
-    last = lax.rem(i + 1, n)
-    relay2(last).wait_recv()
-    relay3(last).start()
+
+    def spread(t):
+        src = lax.rem(i + n - stride(t), n)
+        relay2(src).wait_recv()
+        relay3(src).start()
+
+    ahead = 2
+    for t in range(ahead):
+        answer(t)
+    relay2(i).wait_recv()
+    relay3(i).start()
+
+    def flow(t, carry):
+        answer(t)
+        relay(t - ahead)
+
+        @pl.when(t > ahead)
+        def _():
+            spread(t - ahead - 1)
+        return carry
+
+    lax.fori_loop(ahead, n - 1, flow, 0)
+    for t in range(n - 1 - ahead, n - 1):
+        relay(t)
+        spread(t - 1)
+    spread(n - 2)
 
     def settle(o, carry):
         relay1(o).wait_recv()
@@ -395,7 +413,7 @@
     dma = lambda k: pltpu.SemaphoreType.DMA((k,))
     bf = jnp.bfloat16
     padded = jnp.pad(buckets, ((0, 0), (0, 128 - HG)))
-    hbm = pl.BlockSpec(memory_space=pl.ANY)
+    hbm = pl.BlockSpec(memory_space=pltpu.HBM)
     half = (BLK // 2, 2 * DH)
     items_s, items_v, ball = pl.pallas_call(
         functools.partial(project_kernel, n, nc),

time: 140 us -> 139 us (level)
  Pallas kernels: 129 us -> 127 us
    pallas_call x1, Pallas kernels: 99.4 us -> 97.3 us  [per_device(): pl.pallas_call(functools.partial(attend_kernel, n, cap, nb), out_shape=ja...]
where the time goes in v3:
time: 139 us; the launch traced here: 137 us
  Pallas kernels  127 us (91%)
  local copies, waits for them, and re-layouts  7.77 us (6%)
  other arithmetic  2.89 us (2%)
    pallas_call x1, Pallas kernels, per_device(): pl.pallas_call(functools.partial(attend_kernel, n, cap, nb), out_shape=ja...  97.3 us
    pallas_call x1, Pallas kernels, per_device(): pl.pallas_call(functools.partial(project_kernel, n, nc), out_shape=(jax.S...  29.2 us
    unnamed x14, local copies, waits for them, and re-layouts  6.02 us

profile of v3, /device:TPU:29, one launch (start us, length us, event | category | flops | bytes accessed | tf_op | source)
XLA Modules:
  0.0 137.3 jit_solution(6601391995862027105)
XLA Ops:
  0.0 0.1 add.98
  0.1 0.1 add.93
  0.2 0.0 copy-start.5
  0.2 0.1 add.94
  0.2 0.6 copy-done.5
  0.8 0.1 copy.12
  1.0 0.0 copy-start
  1.0 1.2 copy-done
  2.2 0.0 copy-start.3
  2.2 1.0 copy-done.3
  3.2 0.0 copy-start.4
  3.2 1.0 copy-done.4
  4.3 29.2 %shard_map.55 = (bf16[64,64,128]{2,1,0:T(8,128)(2,1)S(1)}, bf16[64,64,128]{2,1,0:T(8,128)(2,1)S(1)}, s32[4,8,16,128]{3,2,1,0:T(8,128)S(1)}) custom-call(bf16[8,256,256]{2,1,0:T(8,128)(2,1)S(1)} %bitcast.9, s32[16,128]{1,0:T(8,128)S(1)} %pad.4.buck, bf16[1024,256]{1,0:T(8,128)(2,1)S(1)} %copy-done.3, bf16[1024,256]{1,0:T(8,128)(2,1)S(1)} %copy-done.4), custom_call_target="tpu_custom_call" | custom-call | tf_op jit(solution)/shard_map/pallas_call | solution.py:418
  33.4 0.0 copy-start.1
  33.5 0.1 copy.13
  33.6 0.7 convert_reduce_fusion.1
  34.3 0.2 copy.15
  34.4 0.2 reshape.151
  34.7 0.1 squeeze.13
  34.7 0.1 eq.91
  34.8 0.9 convert_reduce_fusion
  35.8 0.5 broadcast.158
  36.3 0.7 fusion.4
  37.0 0.1 squeeze.12
  37.0 0.2 select_reduce_fusion.1
  37.2 0.1 reshape.153
  37.3 0.1 select_reduce_fusion.3
  37.4 0.2 select_reduce_fusion.2
  37.6 0.1 reshape.152
  37.7 0.2 slice_reduce_fusion
  37.9 0.1 pad_add_fusion.idx
  37.9 0.0 copy-done.1
  37.9 0.0 copy-start.2
  37.9 1.0 copy-done.2
  39.0 97.3 %shard_map.56 = bf16[16,128,256]{2,1,0:T(8,128)(2,1)S(1)} custom-call(s32[388]{0:T(512)S(1)} %pad_add_fusion.idx, bf16[64,64,128]{2,1,0:T(8,128)(2,1)S(1)} %get-tuple-element.9.items_s, bf16[64,64,128]{2,1,0:T(8,128)(2,1)S(1)} %get-tuple-element.10.items_v, bf16[16,128,256]{2,1,0:T(8,128)(2,1)S(1)} %bitcast.10, bf16[1024,256]{1,0:T(8,128)(2,1)S(1)} %copy-done.2), custom_call_target="tpu_custom_call" | custom-call | tf_op jit(solution)/shard_map/pallas_call | solution.py:434
  136.3 1.0 copy.17
  (17 shorter events, 0.1 us)
Async XLA Ops:
  0.2 0.7 copy-start.5
  1.0 1.2 copy-start
  2.2 1.0 copy-start.3
  3.2 1.0 copy-start.4
  33.4 4.5 %copy-start.1 = (bf16[2048,256]{1,0:T(8,128)(2,1)S(1)}, bf16[2048,256]{1,0:T(8,128)(2,1)}, u32[]{:S(2)}) copy-start(bf16[2048,256]{1,0:T(8,128)(2,1)} %param.5) | copy-start | bytes 3145732
  37.9 1.0 copy-start.2

commit v4 on v3

--- a/solution.py
+++ b/solution.py
@@ -289,7 +289,8 @@
     relay1(i).start()
 
     def stride(t):
-        return n // 2 + lax.div(t + 1, 2) * (1 - 2 * lax.rem(t, 2))
+        odd = lax.rem(t, 2)
+        return (1 - odd) * (lax.div(t, 2) + 1) + odd * (n - lax.div(t + 1, 2))
 
     def answer(t):
         p = stride(t)
@@ -309,7 +310,7 @@
         relay2(src).wait_recv()
         relay3(src).start()
 
-    ahead = 2
+    ahead = 3
     for t in range(ahead):
         answer(t)
     relay2(i).wait_recv()
@@ -387,12 +388,17 @@
     count = nb * HG
     item = jnp.arange(count, dtype=jnp.int32)
     owner, within = position // nb, position % nb
-    same = owner[..., :, None] == owner[..., None, :]
-    slot = jnp.sum((same & (item[None, :] < item[:, None])).astype(jnp.int32), axis=3)
-    target = lax.dynamic_index_in_dim(owner * cap + slot, i, 1, keepdims=False)
+    earlier = item[None, :] < item[:, None]
+
+    def slot_in(owners):
+        same = owners[:, :, None] == owners[:, None, :]
+        return jnp.sum((same & earlier).astype(jnp.int32), axis=2)
+
+    here = lax.dynamic_index_in_dim(owner, i, 1, keepdims=False)
+    target = here * cap + slot_in(here)
     slot_ids = jnp.arange(slots, dtype=jnp.int32)
     inverse = jnp.sum(jnp.where(target[0][None, :] == slot_ids[:, None], item[None, :], 0), axis=1)
-    place = (jnp.arange(n, dtype=jnp.int32)[:, None] * cap + slot[0]).reshape(-1)
+    place = (jnp.arange(n, dtype=jnp.int32)[:, None] * cap + slot_in(owner[0])).reshape(-1)
     mine = (owner[0] == i).reshape(-1)
     grid = ((item % HG)[None, :] * nb + within[0]).reshape(-1)
     grid_of = jnp.sum(jnp.where(mine & (place == slot_ids[:, None]), grid, 0), axis=1)

time: 139 us -> 134 us (0.964)
  Pallas kernels: 127 us -> 123 us
    pallas_call x1, Pallas kernels: 97.3 us -> 93.5 us  [per_device(): pl.pallas_call(functools.partial(attend_kernel, n, cap, nb), out_shape=ja...]
where the time goes in v4:
time: 134 us; the launch traced here: 132 us
  Pallas kernels  123 us (92%)
  local copies, waits for them, and re-layouts  7.26 us (5%)
  other arithmetic  1.95 us (1%)
    pallas_call x1, Pallas kernels, per_device(): pl.pallas_call(functools.partial(attend_kernel, n, cap, nb), out_shape=ja...  93.5 us
    pallas_call x1, Pallas kernels, per_device(): pl.pallas_call(functools.partial(project_kernel, n, nc), out_shape=(jax.S...  29.2 us
    unnamed x14, local copies, waits for them, and re-layouts  6.09 us

profile of v4, /device:TPU:29, one launch (start us, length us, event | category | flops | bytes accessed | tf_op | source)
XLA Modules:
  0.0 132.0 jit_solution(9194516765047521289)
XLA Ops:
  0.0 0.1 add.94
  0.1 0.0 copy-start.5
  0.1 0.7 copy-done.5
  0.8 0.1 copy.12
  0.9 0.0 copy-start
  0.9 1.2 copy-done
  2.1 0.0 copy-start.3
  2.1 1.0 copy-done.3
  3.1 0.0 copy-start.4
  3.1 1.0 copy-done.4
  4.2 29.2 %shard_map.55 = (bf16[64,64,128]{2,1,0:T(8,128)(2,1)S(1)}, bf16[64,64,128]{2,1,0:T(8,128)(2,1)S(1)}, s32[4,8,16,128]{3,2,1,0:T(8,128)S(1)}) custom-call(bf16[8,256,256]{2,1,0:T(8,128)(2,1)S(1)} %bitcast.12, s32[16,128]{1,0:T(8,128)S(1)} %pad.4.buck, bf16[1024,256]{1,0:T(8,128)(2,1)S(1)} %copy-done.3, bf16[1024,256]{1,0:T(8,128)(2,1)S(1)} %copy-done.4), custom_call_target="tpu_custom_call" | custom-call | tf_op jit(solution)/shard_map/pallas_call | solution.py:424
  33.4 0.0 copy-start.1
  33.4 0.1 copy.13
  33.5 0.7 convert_reduce_fusion
  34.2 0.2 copy.15
  34.4 0.2 reshape.99
  34.6 0.1 squeeze.12
  34.7 0.1 eq.106
  34.8 0.3 convert_reduce_fusion.1
  35.1 0.1 broadcast_add_fusion
  35.2 0.1 add.91
  35.3 0.2 select_reduce_fusion.1
  35.4 0.1 mul.52
  35.5 0.2 convert_reduce_fusion.2
  35.7 0.1 reduce_sum.72
  35.8 0.1 select_reduce_fusion.3
  36.0 0.2 select_reduce_fusion.2
  36.2 0.1 reshape.100
  36.2 0.2 slice_reduce_fusion
  36.4 0.1 pad_add_fusion.idx
  36.5 0.0 copy-done.1
  36.5 0.0 copy-start.2
  36.5 1.0 copy-done.2
  37.6 93.5 %shard_map.56 = bf16[16,128,256]{2,1,0:T(8,128)(2,1)S(1)} custom-call(s32[388]{0:T(512)S(1)} %pad_add_fusion.idx, bf16[64,64,128]{2,1,0:T(8,128)(2,1)S(1)} %get-tuple-element.9.items_s, bf16[64,64,128]{2,1,0:T(8,128)(2,1)S(1)} %get-tuple-element.10.items_v, bf16[16,128,256]{2,1,0:T(8,128)(2,1)S(1)} %bitcast.13, bf16[1024,256]{1,0:T(8,128)(2,1)S(1)} %copy-done.2), custom_call_target="tpu_custom_call" | custom-call | tf_op jit(solution)/shard_map/pallas_call | solution.py:440
  131.1 1.0 copy.17
  (19 shorter events, 0.2 us)
Async XLA Ops:
  0.1 0.7 copy-start.5
  0.9 1.2 copy-start
  2.1 1.0 copy-start.3
  3.1 1.0 copy-start.4
  33.4 3.1 %copy-start.1 = (bf16[2048,256]{1,0:T(8,128)(2,1)S(1)}, bf16[2048,256]{1,0:T(8,128)(2,1)}, u32[]{:S(2)}) copy-start(bf16[2048,256]{1,0:T(8,128)(2,1)} %param.5) | copy-start | bytes 3145732
  36.5 1.0 copy-start.2
